TPU v7x, 32 devices: a whole 2x2x4 slice. The times are simulated.
32 devices in a mesh: grp: 2 (over y), ctx: 4 (over z), head: 2 (over x), rep: 2 (over core).
Axes of the slice: x: 2, y: 2, z: 4, core: 2. Of those that a mesh axis runs over, the one named last changes fastest.
Arguments:
- tokens: bfloat16 [4096, 2048], P(('grp', 'ctx', 'rep')), parts along dimension 0, may hold values from -6 to 6
- doc_ids: int32 [4096], P(('grp', 'ctx', 'rep')), parts along dimension 0, may hold values from 0 to 3, never falling along the last dimension, each value on 1 to 1024 neighbouring positions
- dest_rows: int32 [4096], P(('grp', 'ctx', 'rep')), parts along dimension 0, may hold values from 0 to 2047, as said below
- w_query: bfloat16 [2048, 4096], P(None, 'head'), may hold values from -0.125 to 0.125
- w_key: bfloat16 [2048, 512], P(None, 'head'), may hold values from -0.125 to 0.125
- w_value: bfloat16 [2048, 512], P(None, 'head'), may hold values from -0.125 to 0.125
- w_out: bfloat16 [4096, 2048], P('head'), may hold values from -0.09375 to 0.09375
Outputs:
- layer_out: bfloat16 [4096, 2048], P(('grp', 'ctx', 'rep'), 'head'), parts along dimension 0
There are 2 independent parts, one for each index of `grp`. A program takes and returns all parts, laid end to end along the dimension named above; an argument that names none is the same for every part. Nothing has to cross between parts.
Inputs may be any that keep to these rules, and one draw needn't show every extreme that they name: dest_rows is a permutation of the 2048 rows; owner o holds rows o * 256 to (o + 1) * 256 - 1. The 256 tokens of one device go in runs of 16 consecutive tokens, a run to one owner; each device sends 3 * 16 = 48 tokens to half of the owners and 16 to each of the others. `doc_ids`: document number of each token, never falling along the sequence.
All inputs are finite; a program needn't handle non-finite values.
Results may differ from a plain program's by a relative error of at most 0.0078.
Values may be sent and summed in bfloat16 or wider, within the bound.
No kernel may reach another device: no remote copies, remote signals or barrier semaphores. Data moves between devices by JAX's collectives and lax.ppermute only.
A program may use at most 128 MiB of HBM per device.

v0:
```python
import math
import jax
import jax.numpy as jnp
from jax import lax
from jax.sharding import PartitionSpec as P

HD = 128
THETA = 1000000.0
EPSILON = 1e-06


def rope_tables(positions, head_dim):
    inverse = jnp.power(THETA, -(jnp.arange(0, head_dim, 2, dtype=jnp.float32) / head_dim))
    angles = positions.astype(jnp.float32)[:, None] * inverse[None, :]
    cosine = jnp.cos(angles)
    sine = jnp.sin(angles)
    return (jnp.concatenate([cosine, cosine], -1), jnp.concatenate([sine, sine], -1))


def project_heads(tokens, weight, positions, head_dim):
    flat = jnp.dot(tokens, weight, preferred_element_type=jnp.float32)
    heads = flat.reshape(flat.shape[0], -1, head_dim)
    normed = heads * lax.rsqrt(jnp.mean(heads * heads, axis=-1, keepdims=True) + EPSILON)
    cosine, sine = rope_tables(positions, head_dim)
    half_dim = head_dim // 2
    rotated = jnp.concatenate([-normed[..., half_dim:], normed[..., :half_dim]], -1)
    return (normed * cosine[:, None, :] + rotated * sine[:, None, :]).astype(jnp.bfloat16)


def route_rows(dest_rows, tok_rows):
    owners = lax.axis_size(("ctx", "rep"))
    capacity = 3 * (tok_rows // (2 * owners))
    owner_of = dest_rows // tok_rows
    slot_in = dest_rows - owner_of * tok_rows
    onehot = (owner_of[:, None] == jnp.arange(owners, dtype=jnp.int32)[None, :]).astype(jnp.int32)
    order_in = jnp.sum((jnp.cumsum(onehot, axis=0) - onehot) * onehot, axis=1)
    return (owner_of * capacity + order_in, slot_in, owners * capacity)


def scatter_rows(values, buffer_pos, buffer_len, filler):
    empty = jnp.full((buffer_len,) + values.shape[1:], filler, values.dtype)
    return empty.at[buffer_pos].set(values)


def place_rows(values, slots, tok_rows):
    target = jnp.where(slots >= 0, slots, tok_rows)
    empty = jnp.zeros((tok_rows,) + values.shape[1:], values.dtype)
    return empty.at[target].set(values, mode="drop")


def attend(queries, query_pos, query_seg, keys_in, values_in, key_seg):
    rows_all, kv_heads, groups, head_dim = queries.shape
    score_scale = 1.0 / math.sqrt(head_dim)

    def add_block(totals, key_blk, value_blk, seg_blk, offset):
        key_pos = offset + jnp.arange(key_blk.shape[0], dtype=jnp.int32)
        visible = (seg_blk[None, :] == query_seg[:, None]) & (
            key_pos[None, :] <= query_pos[:, None]
        )

        def compute(current):
            scores = (
                jnp.einsum("rkgd,nkd->rkgn", queries, key_blk, preferred_element_type=jnp.float32)
                * score_scale
            )
            weights = jnp.where(visible[:, None, None, :], jnp.exp(scores), 0.0)
            numer = current[0] + jnp.einsum(
                "rkgn,nkd->rkgd",
                weights.astype(jnp.bfloat16),
                value_blk,
                preferred_element_type=jnp.float32,
            )
            return (numer, current[1] + jnp.sum(weights, axis=-1))

        return lax.cond(jnp.any(visible), compute, lambda current: current, totals)

    initial = (
        jnp.zeros((rows_all, kv_heads, groups, head_dim), jnp.float32),
        jnp.zeros((rows_all, kv_heads, groups), jnp.float32),
    )
    paired = (
        lax.all_gather(keys_in, "rep", axis=0, tiled=True),
        lax.all_gather(values_in, "rep", axis=0, tiled=True),
        lax.all_gather(key_seg, "rep", axis=0, tiled=True),
    )
    key_part = lax.all_gather(paired[0], "ctx", axis=0, tiled=True)
    value_part = lax.all_gather(paired[1], "ctx", axis=0, tiled=True)
    seg_part = lax.all_gather(paired[2], "ctx", axis=0, tiled=True)
    length = key_part.shape[0]
    block_rows = 512
    blocks = length // block_rows

    def loop_body(counter, current):
        first_row = counter * block_rows
        return add_block(
            current,
            lax.dynamic_slice_in_dim(key_part, first_row, block_rows, 0),
            lax.dynamic_slice_in_dim(value_part, first_row, block_rows, 0),
            lax.dynamic_slice_in_dim(seg_part, first_row, block_rows, 0),
            first_row,
        )

    numer, total = lax.fori_loop(0, blocks, loop_body, initial)
    result = numer / total[..., None]
    return result.astype(jnp.bfloat16).reshape(rows_all, kv_heads * groups * head_dim)


def local(tokens, doc_ids, dest_rows, w_query, w_key, w_value, w_out):
    tok_rows = tokens.shape[0]
    head_dim = HD
    positions = lax.axis_index(("ctx", "rep")) * tok_rows + jnp.arange(tok_rows, dtype=jnp.int32)
    queries = project_heads(tokens, w_query, positions, head_dim)
    keys_local = project_heads(tokens, w_key, positions, head_dim)
    kv_heads = keys_local.shape[1]
    groups = queries.shape[1] // kv_heads
    values_local = jnp.dot(tokens, w_value, preferred_element_type=jnp.float32).astype(jnp.bfloat16)
    values_local = values_local.reshape(tok_rows, kv_heads, head_dim)
    buffer_pos, slot_in, buffer_len = route_rows(dest_rows, tok_rows)
    query_flat = queries.reshape(tok_rows, kv_heads * groups * head_dim)
    outgoing = (
        scatter_rows(query_flat, buffer_pos, buffer_len, 0),
        scatter_rows(slot_in, buffer_pos, buffer_len, -1),
        scatter_rows(positions, buffer_pos, buffer_len, 0),
        scatter_rows(doc_ids, buffer_pos, buffer_len, 0),
    )
    got_query, got_slot, got_pos, got_seg = (
        lax.all_to_all(outgoing[0], ("ctx", "rep"), split_axis=0, concat_axis=0, tiled=True),
        lax.all_to_all(outgoing[1], ("ctx", "rep"), split_axis=0, concat_axis=0, tiled=True),
        lax.all_to_all(outgoing[2], ("ctx", "rep"), split_axis=0, concat_axis=0, tiled=True),
        lax.all_to_all(outgoing[3], ("ctx", "rep"), split_axis=0, concat_axis=0, tiled=True),
    )
    own_query = place_rows(got_query, got_slot, tok_rows).reshape(
        tok_rows, kv_heads, groups, head_dim
    )
    own_pos = place_rows(got_pos, got_slot, tok_rows)
    own_seg = place_rows(got_seg, got_slot, tok_rows)
    attended = attend(own_query, own_pos, own_seg, keys_local, values_local, doc_ids)
    partial_out = jnp.dot(attended, w_out, preferred_element_type=jnp.float32).astype(jnp.bfloat16)
    return (
        lax.psum_scatter(partial_out, "head", scatter_dimension=1, tiled=True)
        .astype(jnp.float32)
        .astype(jnp.bfloat16)
    )


def solution(mesh):
    return jax.shard_map(
        local,
        mesh=mesh,
        in_specs=(
            P(("grp", "ctx", "rep"), None),
            P(("grp", "ctx", "rep")),
            P(("grp", "ctx", "rep")),
            P(None, "head"),
            P(None, "head"),
            P(None, "head"),
            P("head", None),
        ),
        out_specs=P(("grp", "ctx", "rep"), "head"),
        check_vma=False,
    )
```

profile of v0, /device:TPU:0, one launch (start us, length us, event | category | flops | bytes accessed | tf_op | source)
XLA Modules:
  0.0 215.8 jit_solution(6226166310934283381)
XLA Ops:
  10.4 6.3 %all-to-all-start = ((s32[8,48,1]{1,2,0:T(1,128)}), s32[8,48,1]{1,2,0:T(1,128)S(1)}, u32[]{:S(2)}, u32[]{:S(2)}) async-start(s32[8,48,1]{1,2,0:T(1,128)} %bitcast.12), calls=%async_computation | async-start | bytes 8192 | tf_op jit(solution)/shard_map/all_to_all | solution.py:128
  19.9 2.2 %all_gather.20 = bf16[512,2,128]{2,0,1:T(8,128)(2,1)} all-gather(bf16[256,2,128]{2,0,1:T(8,128)(2,1)S(1)} %fusion.25), channel_id=1, replica_groups=mesh['grp'=2,'ctx'=4,'head'=2,'rep'=2] {'rep'}, dimensions={0}, use_global_device_ids=true | all-gather | bytes 393216 | tf_op jit(solution)/shard_map/all_gather | solution.py:82
  22.2 5.7 %fusion.42 = f32[256,2048]{1,0:T(8,128)S(1)} fusion(bf16[256,2048]{1,0:T(8,128)(2,1)S(1)} %copy-done, bf16[2048,2048]{1,0:T(8,128)(2,1)} %param.14), kind=kOutput, calls=%fused_computation.83 | convolution fusion | flops 2147483648 | bytes 11534336 | tf_op jit(solution)/shard_map/dot_general | solution.py:21
  31.3 2.2 %broadcast_multiply_fusion = f32[256,16,128]{2,1,0:T(8,128)S(1)} fusion(f32[256,16]{1,0:T(8,128)S(1)} %copy.47, f32[32,8,16,128]{3,2,1,0:T(8,128)} %copy-done.1), kind=kLoop, calls=%fused_computation.37 | loop fusion | flops 524288 | bytes 4210688 | tf_op jit(solution)/shard_map/mul | solution.py:23
  35.7 5.0 %all-to-all-start.2 = ((s32[8,48,1]{1,2,0:T(1,128)}), s32[8,48,1]{1,2,0:T(1,128)S(1)}, u32[]{:S(2)}, u32[]{:S(2)}) async-start(s32[8,48,1]{1,2,0:T(1,128)} %bitcast.14), calls=%async_computation.2 | async-start | bytes 8192 | tf_op jit(solution)/shard_map/all_to_all | solution.py:129
  40.6 2.7 %slice_negate_fusion = (f32[256,16,64]{2,1,0:T(8,128)}, f32[256,16,64]{2,1,0:T(8,128)}) fusion(f32[256,16,128]{2,1,0:T(8,128)S(1)} %broadcast_multiply_fusion), kind=kLoop, calls=%fused_computation.31 | loop fusion | flops 262144 | bytes 4194304 | tf_op jit(solution)/shard_map/neg | solution.py:26
  46.2 4.3 %all-to-all-start.1 = ((s32[8,48,1]{1,2,0:T(1,128)}), s32[8,48,1]{1,2,0:T(1,128)S(1)}, u32[]{:S(2)}, u32[]{:S(2)}) async-start(s32[8,48,1]{1,2,0:T(1,128)} %bitcast.13), calls=%async_computation.1 | async-start | bytes 8192 | tf_op jit(solution)/shard_map/all_to_all | solution.py:130
  50.5 2.8 %maximum_multiply_fusion = f32[256,16,128]{2,1,0:T(8,128)S(1)} fusion(f32[256,16,64]{2,1,0:T(8,128)} %get-tuple-element.300, f32[256,16,64]{2,1,0:T(8,128)} %get-tuple-element.299, f32[256,128]{1,0:T(8,128)S(1)} %pad_maximum_fusion.1), kind=kLoop, calls=%fused_computation.32 | loop fusion | flops 1048576 | bytes 4325376 | tf_op jit(solution)/shard_map/mul | solution.py:27
  54.8 1.9 mul.138
  56.7 7.4 %scatter_custom_fusion.5 = bf16[384,2048]{1,0:T(8,128)(2,1)} fusion(s32[256]{0:T(256)} %copy-done.5, f32[32,8,16,128]{3,2,1,0:T(8,128)S(1)} %bitcast.79, f32[32,8,16,128]{3,2,1,0:T(8,128)} %bitcast.81, f32[256,2048]{1,0:T(8,128)} %copy-done.2, f32[32,8,16,128]{3,2,1,0:T(8,128)} %bitcast.82, bf16[]{:T(256)} %constant.112.clone.1), kind=kCustom, calls=%fused_computation.36 | custom fusion | flops 2097152 | bytes 9961984 | tf_op jit(solution)/shard_map/scatter | solution.py:42
  64.1 5.1 %all-to-all-start.3 = ((bf16[8,48,2048]{2,1,0:T(8,128)(2,1)}), bf16[8,48,2048]{2,1,0:T(8,128)(2,1)S(1)}, u32[]{:S(2)}, u32[]{:S(2)}) async-start(bf16[8,48,2048]{2,1,0:T(8,128)(2,1)} %bitcast.84), calls=%async_computation.3 | async-start | bytes 3145728 | tf_op jit(solution)/shard_map/all_to_all | solution.py:127
  71.1 2.2 %all_gather.22 = bf16[512,2,128]{2,0,1:T(8,128)(2,1)} all-gather(bf16[256,2,128]{2,0,1:T(8,128)(2,1)S(1)} %copy.49), channel_id=1, replica_groups=mesh['grp'=2,'ctx'=4,'head'=2,'rep'=2] {'rep'}, dimensions={0}, use_global_device_ids=true | all-gather | bytes 393216 | tf_op jit(solution)/shard_map/all_gather | solution.py:83
  75.3 53.8 %all-gather.1 = s32[4,1,512]{2,1,0:T(1,128)S(1)} all-gather(s32[1,1,512]{2,1,0:T(1,128)S(1)} %bitcast.91), channel_id=1, replica_groups=mesh['grp'=2,'ctx'=4,'head'=2,'rep'=2] {'ctx'}, dimensions={0}, use_global_device_ids=true | all-gather | bytes 10240 | tf_op jit(solution)/shard_map/all_gather | solution.py:88
  132.0 2.9 %scatter_custom_fusion.4 = s32[256]{0:T(256)S(1)} fusion(s32[384]{0:T(512)S(1)} %fusion.29, s32[384]{0:T(512)S(1)} %reshape.153, s32[]{:T(128)} %constant.95.clone.1), kind=kCustom, calls=%fused_computation.79 | custom fusion | bytes 1028 | tf_op jit(solution)/shard_map/scatter | solution.py:48
  134.9 2.9 %scatter_custom_fusion.2 = s32[256]{0:T(256)S(1)} fusion(s32[384]{0:T(512)S(1)} %fusion.29, s32[384]{0:T(512)S(1)} %reshape.137, s32[]{:T(128)} %constant.95.clone.1), kind=kCustom, calls=%fused_computation.77 | custom fusion | bytes 1028 | tf_op jit(solution)/shard_map/scatter | solution.py:48
  139.0 4.2 %scatter_custom_fusion.6 = bf16[256,2048]{1,0:T(8,128)(2,1)S(1)} fusion(s32[384]{0:T(512)S(1)} %fusion.29, bf16[384,2048]{1,0:T(8,128)(2,1)} %bitcast.86, bf16[]{:T(256)} %constant.112.clone.1), kind=kCustom, calls=%fused_computation.39 | custom fusion | bytes 1049088 | tf_op jit(solution)/shard_map/scatter | solution.py:48
  145.3 34.9 %while.15 = (s32[]{:T(128)}, f32[256,2,8,128]{3,0,2,1:T(8,128)S(1)}, f32[256,2,8]{0,2,1:T(8,128)S(1)}, s32[2048]{0:T(1024)S(1)}, s32[256]{0:T(256)S(1)}, /*index...) while((s32[]{:T(128)}, ...), condition=%wide.region_17.18_spmd, body=%wide.region_12.0_spmd.sunk | while | flops 1087373824 | bytes 23016728 | solution.py:103
  146.9 7.1 %conditional.2 = ((f32[256,2,8,128]{3,0,2,1:T(8,128)S(1)}, f32[256,2,8]{0,2,1:T(8,128)S(1)})) conditional(s32[]{:T(128)} %convert_element_type.67, (f32[256,2,8,128]{3,0,2,1:T(8,128)S(1)}, f32[256,2,8]{0,2,1:T(8,128)S(1)}) %tuple.56, (pred[256,512]{0,1:T(8,128)(4,1)S(1)}, bf16[2048,2,128]{2,0,1:T(8,128)(2,1)}, s32[]{:T(128)}, ...), branch_computations={%region_14.14_spmd, %region_15.16_spmd} | conditional | flops 1086849024 | bytes 22873112 | solution.py:75
  146.9 3.3 %fusion = (f32[256,2,8]{0,2,1:T(8,128)S(1)}, f32[2,512,256,8]{2,1,3,0:T(8,128)S(1)}) fusion(pred[256,512]{0,1:T(8,128)(4,1)S(1)} %get-tuple-element.208, bf16[256,2,8,128]{3,0,2,1:T(8,128)(2,1)} %get-tuple-element.211, bf16[2048,2,128]{2,0,1:T(8,128)(2,1)} %get-tuple-element.209, s32[]{:T(128)} %get-tuple-element.210), kind=kOutput, calls=%fused_computation.8 | convolution fusion | flops 543158272 | bytes 9847296 | tf_op jit(solution)/shard_map/while/body/eval_jaxpr/cond/branch_1_fun/rkgd,nkd->rkgn/dot_general | solution.py:63
  150.2 3.8 %bitcast_add_fusion = f32[256,2,8,128]{3,0,2,1:T(8,128)S(1)} fusion(f32[256,2,8,128]{3,0,2,1:T(8,128)S(1)} %get-tuple-element.207, f32[2,512,256,8]{2,1,3,0:T(8,128)S(1)} %get-tuple-element.298, pred[256,512]{0,1:T(8,128)(4,1)S(1)} %get-tuple-element.208, bf16[2048,2,128]{2,0,1:T(8,128)(2,1)} %get-tuple-element.212, s32[]{:T(128)} %get-tuple-element.210), kind=kOutput, calls=%fused_computation.14 | convolution fusion | flops 543686656 | bytes 12976640 | tf_op jit(solution)/shard_map/while/body/eval_jaxpr/cond/branch_1_fun/rkgn,nkd->rkgd/dot_general | solution.py:67
  155.6 7.1 %conditional.2 = ((f32[256,2,8,128]{3,0,2,1:T(8,128)S(1)}, f32[256,2,8]{0,2,1:T(8,128)S(1)})) conditional(s32[]{:T(128)} %convert_element_type.67, (f32[256,2,8,128]{3,0,2,1:T(8,128)S(1)}, f32[256,2,8]{0,2,1:T(8,128)S(1)}) %tuple.56, (pred[256,512]{0,1:T(8,128)(4,1)S(1)}, bf16[2048,2,128]{2,0,1:T(8,128)(2,1)}, s32[]{:T(128)}, ...), branch_computations={%region_14.14_spmd, %region_15.16_spmd} | conditional | flops 1086849024 | bytes 22873112 | solution.py:75
  155.6 3.3 %fusion = (f32[256,2,8]{0,2,1:T(8,128)S(1)}, f32[2,512,256,8]{2,1,3,0:T(8,128)S(1)}) fusion(pred[256,512]{0,1:T(8,128)(4,1)S(1)} %get-tuple-element.208, bf16[256,2,8,128]{3,0,2,1:T(8,128)(2,1)} %get-tuple-element.211, bf16[2048,2,128]{2,0,1:T(8,128)(2,1)} %get-tuple-element.209, s32[]{:T(128)} %get-tuple-element.210), kind=kOutput, calls=%fused_computation.8 | convolution fusion | flops 543158272 | bytes 9847296 | tf_op jit(solution)/shard_map/while/body/eval_jaxpr/cond/branch_1_fun/rkgd,nkd->rkgn/dot_general | solution.py:63
  158.9 3.8 %bitcast_add_fusion = f32[256,2,8,128]{3,0,2,1:T(8,128)S(1)} fusion(f32[256,2,8,128]{3,0,2,1:T(8,128)S(1)} %get-tuple-element.207, f32[2,512,256,8]{2,1,3,0:T(8,128)S(1)} %get-tuple-element.298, pred[256,512]{0,1:T(8,128)(4,1)S(1)} %get-tuple-element.208, bf16[2048,2,128]{2,0,1:T(8,128)(2,1)} %get-tuple-element.212, s32[]{:T(128)} %get-tuple-element.210), kind=kOutput, calls=%fused_computation.14 | convolution fusion | flops 543686656 | bytes 12976640 | tf_op jit(solution)/shard_map/while/body/eval_jaxpr/cond/branch_1_fun/rkgn,nkd->rkgd/dot_general | solution.py:67
  164.3 7.1 %conditional.2 = ((f32[256,2,8,128]{3,0,2,1:T(8,128)S(1)}, f32[256,2,8]{0,2,1:T(8,128)S(1)})) conditional(s32[]{:T(128)} %convert_element_type.67, (f32[256,2,8,128]{3,0,2,1:T(8,128)S(1)}, f32[256,2,8]{0,2,1:T(8,128)S(1)}) %tuple.56, (pred[256,512]{0,1:T(8,128)(4,1)S(1)}, bf16[2048,2,128]{2,0,1:T(8,128)(2,1)}, s32[]{:T(128)}, ...), branch_computations={%region_14.14_spmd, %region_15.16_spmd} | conditional | flops 1086849024 | bytes 22873112 | solution.py:75
  164.4 3.3 %fusion = (f32[256,2,8]{0,2,1:T(8,128)S(1)}, f32[2,512,256,8]{2,1,3,0:T(8,128)S(1)}) fusion(pred[256,512]{0,1:T(8,128)(4,1)S(1)} %get-tuple-element.208, bf16[256,2,8,128]{3,0,2,1:T(8,128)(2,1)} %get-tuple-element.211, bf16[2048,2,128]{2,0,1:T(8,128)(2,1)} %get-tuple-element.209, s32[]{:T(128)} %get-tuple-element.210), kind=kOutput, calls=%fused_computation.8 | convolution fusion | flops 543158272 | bytes 9847296 | tf_op jit(solution)/shard_map/while/body/eval_jaxpr/cond/branch_1_fun/rkgd,nkd->rkgn/dot_general | solution.py:63
  167.7 3.8 %bitcast_add_fusion = f32[256,2,8,128]{3,0,2,1:T(8,128)S(1)} fusion(f32[256,2,8,128]{3,0,2,1:T(8,128)S(1)} %get-tuple-element.207, f32[2,512,256,8]{2,1,3,0:T(8,128)S(1)} %get-tuple-element.298, pred[256,512]{0,1:T(8,128)(4,1)S(1)} %get-tuple-element.208, bf16[2048,2,128]{2,0,1:T(8,128)(2,1)} %get-tuple-element.212, s32[]{:T(128)} %get-tuple-element.210), kind=kOutput, calls=%fused_computation.14 | convolution fusion | flops 543686656 | bytes 12976640 | tf_op jit(solution)/shard_map/while/body/eval_jaxpr/cond/branch_1_fun/rkgn,nkd->rkgd/dot_general | solution.py:67
  173.1 7.1 %conditional.2 = ((f32[256,2,8,128]{3,0,2,1:T(8,128)S(1)}, f32[256,2,8]{0,2,1:T(8,128)S(1)})) conditional(s32[]{:T(128)} %convert_element_type.67, (f32[256,2,8,128]{3,0,2,1:T(8,128)S(1)}, f32[256,2,8]{0,2,1:T(8,128)S(1)}) %tuple.56, (pred[256,512]{0,1:T(8,128)(4,1)S(1)}, bf16[2048,2,128]{2,0,1:T(8,128)(2,1)}, s32[]{:T(128)}, ...), branch_computations={%region_14.14_spmd, %region_15.16_spmd} | conditional | flops 1086849024 | bytes 22873112 | solution.py:75
  173.1 3.3 %fusion = (f32[256,2,8]{0,2,1:T(8,128)S(1)}, f32[2,512,256,8]{2,1,3,0:T(8,128)S(1)}) fusion(pred[256,512]{0,1:T(8,128)(4,1)S(1)} %get-tuple-element.208, bf16[256,2,8,128]{3,0,2,1:T(8,128)(2,1)} %get-tuple-element.211, bf16[2048,2,128]{2,0,1:T(8,128)(2,1)} %get-tuple-element.209, s32[]{:T(128)} %get-tuple-element.210), kind=kOutput, calls=%fused_computation.8 | convolution fusion | flops 543158272 | bytes 9847296 | tf_op jit(solution)/shard_map/while/body/eval_jaxpr/cond/branch_1_fun/rkgd,nkd->rkgn/dot_general | solution.py:63
  176.4 3.8 %bitcast_add_fusion = f32[256,2,8,128]{3,0,2,1:T(8,128)S(1)} fusion(f32[256,2,8,128]{3,0,2,1:T(8,128)S(1)} %get-tuple-element.207, f32[2,512,256,8]{2,1,3,0:T(8,128)S(1)} %get-tuple-element.298, pred[256,512]{0,1:T(8,128)(4,1)S(1)} %get-tuple-element.208, bf16[2048,2,128]{2,0,1:T(8,128)(2,1)} %get-tuple-element.212, s32[]{:T(128)} %get-tuple-element.210), kind=kOutput, calls=%fused_computation.14 | convolution fusion | flops 543686656 | bytes 12976640 | tf_op jit(solution)/shard_map/while/body/eval_jaxpr/cond/branch_1_fun/rkgn,nkd->rkgd/dot_general | solution.py:67
  180.2 1.9 copy.51
  183.9 6.7 %convolution_convert_fusion = bf16[256,2048]{1,0:T(8,128)(2,1)} fusion(bf16[256,2048]{0,1:T(8,128)(2,1)S(1)} %bitcast.83, bf16[2048,2048]{1,0:T(8,128)(2,1)} %param.17), kind=kOutput, calls=%fused_computation.26 | convolution fusion | flops 2148007936 | bytes 10485760 | tf_op jit(solution)/shard_map/dot_general | solution.py:138
  190.6 18.6 %reduce-scatter.2.cloned.1.call-done = bf16[256,1024]{1,0:T(8,128)(2,1)} async-done(((bf16[256,2048]{1,0:T(8,128)(2,1)}), bf16[256,1024]{1,0:T(8,128)(2,1)}) %reduce-scatter.2.cloned.1.call-update) | async-done | bytes 524304 | tf_op jit(solution)/shard_map/reduce_scatter | solution.py:140
  (87 shorter events, 32.3 us)
Async XLA Ops:
  6.5 11.0 %copy-start = (bf16[256,2048]{1,0:T(8,128)(2,1)S(1)}, bf16[256,2048]{1,0:T(8,128)(2,1)}, u32[]{:S(2)}) copy-start(bf16[256,2048]{1,0:T(8,128)(2,1)} %param.11) | copy-start | bytes 3145732
  8.3 35.1 %copy-start.5 = (s32[256]{0:T(256)}, s32[256]{0:T(256)S(1)}, u32[]{:S(2)}) copy-start(s32[256]{0:T(256)S(1)} %compare_select_fusion.2) | copy-start | bytes 3076
  10.4 25.3 %all-to-all-start = ((s32[8,48,1]{1,2,0:T(1,128)}), s32[8,48,1]{1,2,0:T(1,128)S(1)}, u32[]{:S(2)}, u32[]{:S(2)}) async-start(s32[8,48,1]{1,2,0:T(1,128)} %bitcast.12), calls=%async_computation | async-start | bytes 8192 | tf_op jit(solution)/shard_map/all_to_all | solution.py:128
  16.7 128.4 %all-gather.5.cloned.1.call-start = ((), (), s32[]{:S(2)}) async-start(), calls=%async_computation.5 | async-start | bytes 1310720 | tf_op jit(solution)/shard_map/all_gather | solution.py:86
  27.9 1.4 copy-start.2
  29.2 1.3 copy-start.1
  35.7 10.5 %all-to-all-start.2 = ((s32[8,48,1]{1,2,0:T(1,128)}), s32[8,48,1]{1,2,0:T(1,128)S(1)}, u32[]{:S(2)}, u32[]{:S(2)}) async-start(s32[8,48,1]{1,2,0:T(1,128)} %bitcast.14), calls=%async_computation.2 | async-start | bytes 8192 | tf_op jit(solution)/shard_map/all_to_all | solution.py:129
  40.6 2.7 %copy-start.4 = (s32[256]{0:T(256)S(1)}, s32[256]{0:T(256)}, u32[]{:S(2)}) copy-start(s32[256]{0:T(256)} %param.12) | copy-start | bytes 3076
  46.2 17.9 %all-to-all-start.1 = ((s32[8,48,1]{1,2,0:T(1,128)}), s32[8,48,1]{1,2,0:T(1,128)S(1)}, u32[]{:S(2)}, u32[]{:S(2)}) async-start(s32[8,48,1]{1,2,0:T(1,128)} %bitcast.13), calls=%async_computation.1 | async-start | bytes 8192 | tf_op jit(solution)/shard_map/all_to_all | solution.py:130
  64.1 73.7 %all-to-all-start.3 = ((bf16[8,48,2048]{2,1,0:T(8,128)(2,1)}), bf16[8,48,2048]{2,1,0:T(8,128)(2,1)S(1)}, u32[]{:S(2)}, u32[]{:S(2)}) async-start(bf16[8,48,2048]{2,1,0:T(8,128)(2,1)} %bitcast.84), calls=%async_computation.3 | async-start | bytes 3145728 | tf_op jit(solution)/shard_map/all_to_all | solution.py:127
  69.2 75.8 %all-gather.7.cloned.1.call-start = ((), (), s32[]{:S(2)}) async-start(), calls=%async_computation.6 | async-start | bytes 1310720 | tf_op jit(solution)/shard_map/all_gather | solution.py:87
  73.4 135.9 %reduce-scatter.2.cloned.1.call-start = ((), (), s32[]{:S(2)}) async-start(), calls=%async_computation.7 | async-start | bytes 1572864 | tf_op jit(solution)/shard_map/reduce_scatter | solution.py:140
  137.9 1.2 copy-start.3
Sparse Core Ops, SparseCore 0:
  22.3 29.3 all-gather.4
  73.5 49.1 all-gather.6
  190.8 18.4 reduce-scatter.1
where the time goes:
time: 217 us; the launch traced here: 216 us
  blocking collectives  60 us (28%)
  matrix products  44.3 us (20%)
  local copies, waits for them, and re-layouts  29 us (13%)
  other arithmetic  25.9 us (12%)
  starting transfers between devices  20.8 us (10%)
  waiting for transfers between devices  19.4 us (9%)
  between operations  13.4 us (6%)
  loops' own time  2.83 us (1%)
    all_gather x1, blocking collectives, attend(): seg_part = lax.all_gather(paired[2], 'ctx', axis=0, tiled=True)  53.8 us
    reduce_scatter x1, waiting for transfers between devices, local(): lax.psum_scatter(partial_out, 'head', scatter_dimension=1, tiled=True)  18.6 us
    dot_general x4, matrix products, compute(): jnp.einsum('rkgn,nkd->rkgd', weights.astype(jnp.bfloat16), value_blk, pre...  15.1 us
    dot_general x4, matrix products, compute(): jnp.einsum('rkgd,nkd->rkgn', queries, key_blk, preferred_element_type=jnp...  13.2 us
    scatter x4, local copies, waits for them, and re-layouts, place_rows(): return empty.at[target].set(values, mode='drop')  10.5 us
    dot_general x2, matrix products, project_heads(): flat = jnp.dot(tokens, weight, preferred_element_type=jnp.float32)  7.48 us
    scatter x1, other arithmetic, scatter_rows(): return empty.at[buffer_pos].set(values)  7.38 us
    dot_general x1, matrix products, local(): jnp.dot(attended, w_out, preferred_element_type=jnp.float32)  6.74 us
  transfers between devices with their start and end apart: 7, of which 2 were waited for; matrix products, arithmetic and copies ran while one was open for 22% of the time, Pallas kernels for 0%

commit v1 on v0

--- a/solution.py
+++ b/solution.py
@@ -7,6 +7,29 @@
 HD = 128
 THETA = 1000000.0
 EPSILON = 1e-06
+
+
+def cut_along(x, dim, count):
+    before, after = (x.shape[:dim], x.shape[dim + 1 :])
+    return jnp.moveaxis(x.reshape(*before, count, -1, *after), dim, 0)
+
+
+def joined_along(blocks, dim):
+    blocks = jnp.moveaxis(blocks, 0, dim)
+    dims = blocks.shape
+    return blocks.reshape(*dims[:dim], dims[dim] * dims[dim + 1], *dims[dim + 2 :])
+
+
+def rotated_exchange(value, axis, split_dim, concat_dim):
+    size, place = (lax.axis_size(axis), lax.axis_index(axis))
+    pieces = cut_along(value, split_dim, size)
+    out = pieces
+    for step in range(1, size):
+        target, source = ((place + step) % size, (place - step) % size)
+        sent = lax.dynamic_index_in_dim(pieces, target, 0)
+        other = lax.ppermute(sent, axis, [(i, (i + step) % size) for i in range(size)])
+        out = lax.dynamic_update_slice_in_dim(out, other, source, axis=0)
+    return joined_along(out, concat_dim)
 
 
 def rope_tables(positions, head_dim):
@@ -124,7 +147,7 @@
         scatter_rows(doc_ids, buffer_pos, buffer_len, 0),
     )
     got_query, got_slot, got_pos, got_seg = (
-        lax.all_to_all(outgoing[0], ("ctx", "rep"), split_axis=0, concat_axis=0, tiled=True),
+        rotated_exchange(outgoing[0], ("ctx", "rep"), 0, 0),
         lax.all_to_all(outgoing[1], ("ctx", "rep"), split_axis=0, concat_axis=0, tiled=True),
         lax.all_to_all(outgoing[2], ("ctx", "rep"), split_axis=0, concat_axis=0, tiled=True),
         lax.all_to_all(outgoing[3], ("ctx", "rep"), split_axis=0, concat_axis=0, tiled=True),

time: 217 us -> 206 us (0.949)
  blocking collectives: 60 us -> 20.8 us
  waiting for transfers between devices: 19.4 us -> 49.9 us
  local copies, waits for them, and re-layouts: 29 us -> 32.7 us
  other arithmetic: 25.9 us -> 22.8 us
  starting transfers between devices: 20.8 us -> 18.6 us
    all_gather x1, blocking collectives: 53.8 us -> 12.4 us  [attend(): seg_part = lax.all_gather(paired[2], 'ctx', axis=0, tiled=True)]
    ppermute x0 -> x7, waiting for transfers between devices: none -> 14.4 us  [rotated_exchange(): lax.ppermute(sent, axis, [(i, (i + step) % size) for i in range(size)])]
    reduce_scatter x1, waiting for transfers between devices: 18.6 us -> 30.5 us  [local(): lax.psum_scatter(partial_out, 'head', scatter_dimension=1, tiled=True)]
    ppermute x0 -> x7, starting transfers between devices: none -> 7.11 us  [rotated_exchange(): lax.ppermute(sent, axis, [(i, (i + step) % size) for i in range(size)])]
    all_to_all x1 -> x0, starting transfers between devices: 5.1 us -> none  [local(): lax.all_to_all(outgoing[0], ('ctx', 'rep'), split_axis=0, concat_axis=0,...]
    all_to_all x1, waiting for transfers between devices: 0.01 us -> 3.33 us  [local(): lax.all_to_all(outgoing[1], ('ctx', 'rep'), split_axis=0, concat_axis=0,...]
    dynamic_slice x0 -> x2, local copies, waits for them, and re-layouts: none -> 2.87 us  [rotated_exchange(): sent = lax.dynamic_index_in_dim(pieces, target, 0)]
    mul x1, other arithmetic: 2.83 us -> 0.61 us  [project_heads(): rotated * sine[:, None, :]]
  transfers between devices with their start and end apart: 7 -> 13, of which waited for: 2 -> 6; matrix products, arithmetic and copies ran while one was open for 22% -> 24% of each run, Pallas kernels for 0% -> 0%
where the time goes in v1:
time: 206 us; the launch traced here: 205 us
  waiting for transfers between devices  49.9 us (24%)
  matrix products  44.2 us (21%)
  local copies, waits for them, and re-layouts  32.7 us (16%)
  other arithmetic  22.8 us (11%)
  blocking collectives  20.8 us (10%)
  starting transfers between devices  18.6 us (9%)
  between operations  13.6 us (7%)
  loops' own time  2.76 us (1%)
    reduce_scatter x1, waiting for transfers between devices, local(): lax.psum_scatter(partial_out, 'head', scatter_dimension=1, tiled=True)  30.5 us
    dot_general x4, matrix products, compute(): jnp.einsum('rkgn,nkd->rkgd', weights.astype(jnp.bfloat16), value_blk, pre...  15.1 us
    ppermute x7, waiting for transfers between devices, rotated_exchange(): lax.ppermute(sent, axis, [(i, (i + step) % size) for i in range(size)])  14.4 us
    dot_general x4, matrix products, compute(): jnp.einsum('rkgd,nkd->rkgn', queries, key_blk, preferred_element_type=jnp...  13.1 us
    all_gather x1, blocking collectives, attend(): seg_part = lax.all_gather(paired[2], 'ctx', axis=0, tiled=True)  12.4 us
    scatter x4, local copies, waits for them, and re-layouts, place_rows(): return empty.at[target].set(values, mode='drop')  11.2 us
    dot_general x2, matrix products, project_heads(): flat = jnp.dot(tokens, weight, preferred_element_type=jnp.float32)  7.47 us
    scatter x1, other arithmetic, scatter_rows(): return empty.at[buffer_pos].set(values)  7.41 us
  transfers between devices with their start and end apart: 13, of which 6 were waited for; matrix products, arithmetic and copies ran while one was open for 24% of the time, Pallas kernels for 0%

profile of v1, /device:TPU:0, one launch (start us, length us, event | category | flops | bytes accessed | tf_op | source)
XLA Modules:
  0.0 205.5 jit_solution(6421526866080281310)
XLA Ops:
  10.3 2.2 %all_gather.20 = bf16[512,2,128]{2,0,1:T(8,128)(2,1)} all-gather(bf16[256,2,128]{2,0,1:T(8,128)(2,1)S(1)} %fusion.25), channel_id=1, replica_groups=mesh['grp'=2,'ctx'=4,'head'=2,'rep'=2] {'rep'}, dimensions={0}, use_global_device_ids=true | all-gather | bytes 393216 | tf_op jit(solution)/shard_map/all_gather | solution.py:105
  12.6 5.7 %fusion.42 = f32[256,2048]{1,0:T(8,128)S(1)} fusion(bf16[256,2048]{1,0:T(8,128)(2,1)S(1)} %copy-done, bf16[2048,2048]{1,0:T(8,128)(2,1)} %param.14), kind=kOutput, calls=%fused_computation.97 | convolution fusion | flops 2147483648 | bytes 11534336 | tf_op jit(solution)/shard_map/dot_general | solution.py:44
  29.2 1.9 mul.139
  31.2 7.4 %scatter_custom_fusion.5 = bf16[384,2048]{1,0:T(8,128)(2,1)} fusion(s32[256]{0:T(256)S(1)} %compare_select_fusion.2, f32[32,8,16,128]{3,2,1,0:T(8,128)S(1)} %bitcast.79, f32[32,8,16,128]{3,2,1,0:T(8,128)} %bitcast.81, f32[256,2048]{1,0:T(8,128)} %copy-done.1, f32[32,8,16,128]{3,2,1,0:T(8,128)} %bitcast.82, bf16[]{:T(256)} %constant.203.clone.1), kind=kCustom, calls=%fused_computation.36 | custom fusion | flops 2097152 | bytes 9961474 | tf_op jit(solution)/shard_map/scatter | solution.py:65
  42.1 4.4 %all_gather.22 = bf16[512,2,128]{2,0,1:T(8,128)(2,1)} all-gather(bf16[256,2,128]{2,0,1:T(8,128)(2,1)S(1)} %copy.49), channel_id=1, replica_groups=mesh['grp'=2,'ctx'=4,'head'=2,'rep'=2] {'rep'}, dimensions={0}, use_global_device_ids=true | all-gather | bytes 393216 | tf_op jit(solution)/shard_map/all_gather | solution.py:106
  52.4 4.8 %all-to-all-start = ((s32[8,48,1]{1,2,0:T(1,128)}), s32[8,48,1]{1,2,0:T(1,128)S(1)}, u32[]{:S(2)}, u32[]{:S(2)}) async-start(s32[8,48,1]{1,2,0:T(1,128)} %bitcast.12), calls=%async_computation | async-start | bytes 8192 | tf_op jit(solution)/shard_map/all_to_all | solution.py:151
  59.4 3.3 %all-to-all-done = s32[8,48,1]{1,2,0:T(1,128)S(1)} async-done(((s32[8,48,1]{1,2,0:T(1,128)}), s32[8,48,1]{1,2,0:T(1,128)S(1)}, u32[]{:S(2)}, u32[]{:S(2)}) %all-to-all-start) | async-done | bytes 1568 | tf_op jit(solution)/shard_map/all_to_all | solution.py:151
  62.8 3.3 %all-to-all-start.2 = ((s32[8,48,1]{1,2,0:T(1,128)}), s32[8,48,1]{1,2,0:T(1,128)S(1)}, u32[]{:S(2)}, u32[]{:S(2)}) async-start(s32[8,48,1]{1,2,0:T(1,128)} %bitcast.14), calls=%async_computation.2 | async-start | bytes 8192 | tf_op jit(solution)/shard_map/all_to_all | solution.py:152
  71.6 3.4 %all-to-all-start.1 = ((s32[8,48,1]{1,2,0:T(1,128)}), s32[8,48,1]{1,2,0:T(1,128)S(1)}, u32[]{:S(2)}, u32[]{:S(2)}) async-start(s32[8,48,1]{1,2,0:T(1,128)} %bitcast.13), calls=%async_computation.1 | async-start | bytes 8192 | tf_op jit(solution)/shard_map/all_to_all | solution.py:153
  75.0 12.4 %all-gather.1 = s32[4,1,512]{2,1,0:T(1,128)S(1)} all-gather(s32[1,1,512]{2,1,0:T(1,128)S(1)} %bitcast.92), channel_id=1, replica_groups=mesh['grp'=2,'ctx'=4,'head'=2,'rep'=2] {'ctx'}, dimensions={0}, use_global_device_ids=true | all-gather | bytes 10240 | tf_op jit(solution)/shard_map/all_gather | solution.py:111
  90.1 2.9 %scatter_custom_fusion.4 = s32[256]{0:T(256)S(1)} fusion(s32[384]{0:T(512)S(1)} %fusion.29, s32[384]{0:T(512)S(1)} %reshape.159, s32[]{:T(128)} %constant.186.clone.1), kind=kCustom, calls=%fused_computation.93 | custom fusion | bytes 1028 | tf_op jit(solution)/shard_map/scatter | solution.py:71
  93.0 2.9 %scatter_custom_fusion.2 = s32[256]{0:T(256)S(1)} fusion(s32[384]{0:T(512)S(1)} %fusion.29, s32[384]{0:T(512)S(1)} %reshape.143, s32[]{:T(128)} %constant.186.clone.1), kind=kCustom, calls=%fused_computation.91 | custom fusion | bytes 1028 | tf_op jit(solution)/shard_map/scatter | solution.py:71
  97.0 2.3 %collective-permute-start.4 = (bf16[1,48,2048]{2,1,0:T(8,128)(2,1)S(1)}, bf16[1,48,2048]{2,1,0:T(8,128)(2,1)S(1)}, u32[]{:S(2)}, u32[]{:S(2)}) collective-permute-start(bf16[1,48,2048]{2,1,0:T(8,128)(2,1)S(1)} %get-tuple-element.303), channel_id=1, source_target_pairs={{0,9},{1,12},{4,13},{5,0},{8,1},{9,4},{12,5},{13,8},{2,11},{3,14},... | collective-permute-start | bytes 589832 | tf_op jit(solution)/shard_map/ppermute | solution.py:30
  99.3 2.9 %collective-permute-start.5 = (bf16[1,48,2048]{2,1,0:T(8,128)(2,1)S(1)}, bf16[1,48,2048]{2,1,0:T(8,128)(2,1)S(1)}, u32[]{:S(2)}, u32[]{:S(2)}) collective-permute-start(bf16[1,48,2048]{2,1,0:T(8,128)(2,1)S(1)} %get-tuple-element.302), channel_id=1, source_target_pairs={{0,12},{1,13},{4,0},{5,1},{8,4},{9,5},{12,8},{13,9},{2,14},{3,15},... | collective-permute-start | bytes 589832 | tf_op jit(solution)/shard_map/ppermute | solution.py:30
  103.1 11.3 %collective-permute-done.2 = bf16[1,48,2048]{2,1,0:T(8,128)(2,1)S(1)} collective-permute-done((bf16[1,48,2048]{2,1,0:T(8,128)(2,1)}, bf16[1,48,2048]{2,1,0:T(8,128)(2,1)S(1)}, u32[]{:S(2)}, u32[]{:S(2)}) %collective-permute-start.2) | collective-permute-done | bytes 196640 | tf_op jit(solution)/shard_map/ppermute | solution.py:30
  116.3 3.9 %scatter_custom_fusion.6 = bf16[256,2048]{1,0:T(8,128)(2,1)} fusion(s32[384]{0:T(512)S(1)} %fusion.29, bf16[384,2048]{1,0:T(8,128)(2,1)S(1)} %bitcast.86, bf16[]{:T(256)} %constant.203.clone.1), kind=kCustom, calls=%fused_computation.39 | custom fusion | bytes 1048578 | tf_op jit(solution)/shard_map/scatter | solution.py:71
  123.2 34.7 %while.15 = (s32[]{:T(128)}, f32[256,2,8,128]{3,0,2,1:T(8,128)S(1)}, f32[256,2,8]{0,2,1:T(8,128)S(1)}, s32[2048]{0:T(1024)S(1)}, s32[256]{0:T(256)S(1)}, /*index...) while((s32[]{:T(128)}, ...), condition=%wide.region_17.18_spmd, body=%wide.region_12.17_spmd.sunk | while | flops 1087373824 | bytes 23016728 | solution.py:126
  124.8 7.1 %conditional.2 = ((f32[256,2,8,128]{3,0,2,1:T(8,128)S(1)}, f32[256,2,8]{0,2,1:T(8,128)S(1)})) conditional(s32[]{:T(128)} %convert_element_type.67, (f32[256,2,8,128]{3,0,2,1:T(8,128)S(1)}, f32[256,2,8]{0,2,1:T(8,128)S(1)}) %tuple.62, (pred[256,512]{0,1:T(8,128)(4,1)S(1)}, bf16[2048,2,128]{2,0,1:T(8,128)(2,1)}, s32[]{:T(128)}, ...), branch_computations={%region_14.14_spmd, %region_15.16_spmd} | conditional | flops 1086849024 | bytes 22873112 | solution.py:98
  124.8 3.3 %fusion = (f32[256,2,8]{0,2,1:T(8,128)S(1)}, f32[2,512,256,8]{2,1,3,0:T(8,128)S(1)}) fusion(pred[256,512]{0,1:T(8,128)(4,1)S(1)} %get-tuple-element.208, bf16[256,2,8,128]{3,0,2,1:T(8,128)(2,1)} %get-tuple-element.211, bf16[2048,2,128]{2,0,1:T(8,128)(2,1)} %get-tuple-element.209, s32[]{:T(128)} %get-tuple-element.210), kind=kOutput, calls=%fused_computation.8 | convolution fusion | flops 543158272 | bytes 9847296 | tf_op jit(solution)/shard_map/while/body/eval_jaxpr/cond/branch_1_fun/rkgd,nkd->rkgn/dot_general | solution.py:86
  128.1 3.8 %bitcast_add_fusion = f32[256,2,8,128]{3,0,2,1:T(8,128)S(1)} fusion(f32[256,2,8,128]{3,0,2,1:T(8,128)S(1)} %get-tuple-element.207, f32[2,512,256,8]{2,1,3,0:T(8,128)S(1)} %get-tuple-element.298, pred[256,512]{0,1:T(8,128)(4,1)S(1)} %get-tuple-element.208, bf16[2048,2,128]{2,0,1:T(8,128)(2,1)} %get-tuple-element.212, s32[]{:T(128)} %get-tuple-element.210), kind=kOutput, calls=%fused_computation.14 | convolution fusion | flops 543686656 | bytes 12976640 | tf_op jit(solution)/shard_map/while/body/eval_jaxpr/cond/branch_1_fun/rkgn,nkd->rkgd/dot_general | solution.py:90
  133.5 7.1 %conditional.2 = ((f32[256,2,8,128]{3,0,2,1:T(8,128)S(1)}, f32[256,2,8]{0,2,1:T(8,128)S(1)})) conditional(s32[]{:T(128)} %convert_element_type.67, (f32[256,2,8,128]{3,0,2,1:T(8,128)S(1)}, f32[256,2,8]{0,2,1:T(8,128)S(1)}) %tuple.62, (pred[256,512]{0,1:T(8,128)(4,1)S(1)}, bf16[2048,2,128]{2,0,1:T(8,128)(2,1)}, s32[]{:T(128)}, ...), branch_computations={%region_14.14_spmd, %region_15.16_spmd} | conditional | flops 1086849024 | bytes 22873112 | solution.py:98
  133.5 3.3 %fusion = (f32[256,2,8]{0,2,1:T(8,128)S(1)}, f32[2,512,256,8]{2,1,3,0:T(8,128)S(1)}) fusion(pred[256,512]{0,1:T(8,128)(4,1)S(1)} %get-tuple-element.208, bf16[256,2,8,128]{3,0,2,1:T(8,128)(2,1)} %get-tuple-element.211, bf16[2048,2,128]{2,0,1:T(8,128)(2,1)} %get-tuple-element.209, s32[]{:T(128)} %get-tuple-element.210), kind=kOutput, calls=%fused_computation.8 | convolution fusion | flops 543158272 | bytes 9847296 | tf_op jit(solution)/shard_map/while/body/eval_jaxpr/cond/branch_1_fun/rkgd,nkd->rkgn/dot_general | solution.py:86
  136.8 3.8 %bitcast_add_fusion = f32[256,2,8,128]{3,0,2,1:T(8,128)S(1)} fusion(f32[256,2,8,128]{3,0,2,1:T(8,128)S(1)} %get-tuple-element.207, f32[2,512,256,8]{2,1,3,0:T(8,128)S(1)} %get-tuple-element.298, pred[256,512]{0,1:T(8,128)(4,1)S(1)} %get-tuple-element.208, bf16[2048,2,128]{2,0,1:T(8,128)(2,1)} %get-tuple-element.212, s32[]{:T(128)} %get-tuple-element.210), kind=kOutput, calls=%fused_computation.14 | convolution fusion | flops 543686656 | bytes 12976640 | tf_op jit(solution)/shard_map/while/body/eval_jaxpr/cond/branch_1_fun/rkgn,nkd->rkgd/dot_general | solution.py:90
  142.2 7.1 %conditional.2 = ((f32[256,2,8,128]{3,0,2,1:T(8,128)S(1)}, f32[256,2,8]{0,2,1:T(8,128)S(1)})) conditional(s32[]{:T(128)} %convert_element_type.67, (f32[256,2,8,128]{3,0,2,1:T(8,128)S(1)}, f32[256,2,8]{0,2,1:T(8,128)S(1)}) %tuple.62, (pred[256,512]{0,1:T(8,128)(4,1)S(1)}, bf16[2048,2,128]{2,0,1:T(8,128)(2,1)}, s32[]{:T(128)}, ...), branch_computations={%region_14.14_spmd, %region_15.16_spmd} | conditional | flops 1086849024 | bytes 22873112 | solution.py:98
  142.2 3.3 %fusion = (f32[256,2,8]{0,2,1:T(8,128)S(1)}, f32[2,512,256,8]{2,1,3,0:T(8,128)S(1)}) fusion(pred[256,512]{0,1:T(8,128)(4,1)S(1)} %get-tuple-element.208, bf16[256,2,8,128]{3,0,2,1:T(8,128)(2,1)} %get-tuple-element.211, bf16[2048,2,128]{2,0,1:T(8,128)(2,1)} %get-tuple-element.209, s32[]{:T(128)} %get-tuple-element.210), kind=kOutput, calls=%fused_computation.8 | convolution fusion | flops 543158272 | bytes 9847296 | tf_op jit(solution)/shard_map/while/body/eval_jaxpr/cond/branch_1_fun/rkgd,nkd->rkgn/dot_general | solution.py:86
  145.5 3.8 %bitcast_add_fusion = f32[256,2,8,128]{3,0,2,1:T(8,128)S(1)} fusion(f32[256,2,8,128]{3,0,2,1:T(8,128)S(1)} %get-tuple-element.207, f32[2,512,256,8]{2,1,3,0:T(8,128)S(1)} %get-tuple-element.298, pred[256,512]{0,1:T(8,128)(4,1)S(1)} %get-tuple-element.208, bf16[2048,2,128]{2,0,1:T(8,128)(2,1)} %get-tuple-element.212, s32[]{:T(128)} %get-tuple-element.210), kind=kOutput, calls=%fused_computation.14 | convolution fusion | flops 543686656 | bytes 12976640 | tf_op jit(solution)/shard_map/while/body/eval_jaxpr/cond/branch_1_fun/rkgn,nkd->rkgd/dot_general | solution.py:90
  150.9 7.1 %conditional.2 = ((f32[256,2,8,128]{3,0,2,1:T(8,128)S(1)}, f32[256,2,8]{0,2,1:T(8,128)S(1)})) conditional(s32[]{:T(128)} %convert_element_type.67, (f32[256,2,8,128]{3,0,2,1:T(8,128)S(1)}, f32[256,2,8]{0,2,1:T(8,128)S(1)}) %tuple.62, (pred[256,512]{0,1:T(8,128)(4,1)S(1)}, bf16[2048,2,128]{2,0,1:T(8,128)(2,1)}, s32[]{:T(128)}, ...), branch_computations={%region_14.14_spmd, %region_15.16_spmd} | conditional | flops 1086849024 | bytes 22873112 | solution.py:98
  150.9 3.3 %fusion = (f32[256,2,8]{0,2,1:T(8,128)S(1)}, f32[2,512,256,8]{2,1,3,0:T(8,128)S(1)}) fusion(pred[256,512]{0,1:T(8,128)(4,1)S(1)} %get-tuple-element.208, bf16[256,2,8,128]{3,0,2,1:T(8,128)(2,1)} %get-tuple-element.211, bf16[2048,2,128]{2,0,1:T(8,128)(2,1)} %get-tuple-element.209, s32[]{:T(128)} %get-tuple-element.210), kind=kOutput, calls=%fused_computation.8 | convolution fusion | flops 543158272 | bytes 9847296 | tf_op jit(solution)/shard_map/while/body/eval_jaxpr/cond/branch_1_fun/rkgd,nkd->rkgn/dot_general | solution.py:86
  154.2 3.8 %bitcast_add_fusion = f32[256,2,8,128]{3,0,2,1:T(8,128)S(1)} fusion(f32[256,2,8,128]{3,0,2,1:T(8,128)S(1)} %get-tuple-element.207, f32[2,512,256,8]{2,1,3,0:T(8,128)S(1)} %get-tuple-element.298, pred[256,512]{0,1:T(8,128)(4,1)S(1)} %get-tuple-element.208, bf16[2048,2,128]{2,0,1:T(8,128)(2,1)} %get-tuple-element.212, s32[]{:T(128)} %get-tuple-element.210), kind=kOutput, calls=%fused_computation.14 | convolution fusion | flops 543686656 | bytes 12976640 | tf_op jit(solution)/shard_map/while/body/eval_jaxpr/cond/branch_1_fun/rkgn,nkd->rkgd/dot_general | solution.py:90
  158.0 1.9 copy.51
  161.7 6.7 %convolution_convert_fusion = bf16[256,2048]{1,0:T(8,128)(2,1)} fusion(bf16[256,2048]{0,1:T(8,128)(2,1)S(1)} %bitcast.83, bf16[2048,2048]{1,0:T(8,128)(2,1)} %param.17), kind=kOutput, calls=%fused_computation.26 | convolution fusion | flops 2148007936 | bytes 10485760 | tf_op jit(solution)/shard_map/dot_general | solution.py:161
  168.4 30.5 %reduce-scatter.2.cloned.1.call-done = bf16[256,1024]{1,0:T(8,128)(2,1)} async-done(((bf16[256,2048]{1,0:T(8,128)(2,1)}), bf16[256,1024]{1,0:T(8,128)(2,1)}) %reduce-scatter.2.cloned.1.call-update) | async-done | bytes 524304 | tf_op jit(solution)/shard_map/reduce_scatter | solution.py:163
  (105 shorter events, 46.6 us)
Async XLA Ops:
  6.5 1.3 copy-start
  6.5 116.5 %all-gather.5.cloned.1.call-start = ((), (), s32[]{:S(2)}) async-start(), calls=%async_computation.4 | async-start | bytes 1310720 | tf_op jit(solution)/shard_map/all_gather | solution.py:109
  12.5 110.5 %all-gather.7.cloned.1.call-start = ((), (), s32[]{:S(2)}) async-start(), calls=%async_computation.5 | async-start | bytes 1310720 | tf_op jit(solution)/shard_map/all_gather | solution.py:110
  18.3 1.4 copy-start.1
  23.0 0.6 copy-start.3
  38.6 9.5 %copy-start.2 = (bf16[384,2048]{1,0:T(8,128)(2,1)S(1)}, bf16[384,2048]{1,0:T(8,128)(2,1)}, u32[]{:S(2)}) copy-start(bf16[384,2048]{1,0:T(8,128)(2,1)} %scatter_custom_fusion.5) | copy-start | bytes 4718596
  39.6 8.4 %collective-permute-start = (bf16[1,48,2048]{2,1,0:T(8,128)(2,1)S(1)}, bf16[1,48,2048]{2,1,0:T(8,128)(2,1)}, u32[]{:S(2)}, u32[]{:S(2)}) collective-permute-start(bf16[1,48,2048]{2,1,0:T(8,128)(2,1)S(1)} %constant_dynamic-slice_fusion.6), channel_id=1, source_target_pairs={{0,1},{1,4},{4,5},{5,8},{8,9},{9,12},{12,13},{13,0},{2,3},{3,6},{6... | collective-permute-start | bytes 589832 | tf_op jit(solution)/shard_map/ppermute | solution.py:30
  42.0 24.1 %copy-start.4 = (s32[256]{0:T(256)S(1)}, s32[256]{0:T(256)}, u32[]{:S(2)}) copy-start(s32[256]{0:T(256)} %param.12) | copy-start | bytes 3076
  49.9 52.3 %collective-permute-start.1 = (bf16[1,48,2048]{2,1,0:T(8,128)(2,1)}, bf16[1,48,2048]{2,1,0:T(8,128)(2,1)}, u32[]{:S(2)}, u32[]{:S(2)}) collective-permute-start(bf16[1,48,2048]{2,1,0:T(8,128)(2,1)} %get-tuple-element.306), channel_id=1, source_target_pairs={{0,4},{1,5},{4,8},{5,9},{8,12},{9,13},{12,0},{13,1},{2,6},{3,7},{6... | collective-permute-start | bytes 589832 | tf_op jit(solution)/shard_map/ppermute | solution.py:30
  52.4 10.4 %all-to-all-start = ((s32[8,48,1]{1,2,0:T(1,128)}), s32[8,48,1]{1,2,0:T(1,128)S(1)}, u32[]{:S(2)}, u32[]{:S(2)}) async-start(s32[8,48,1]{1,2,0:T(1,128)} %bitcast.12), calls=%async_computation | async-start | bytes 8192 | tf_op jit(solution)/shard_map/all_to_all | solution.py:151
  62.8 8.8 %all-to-all-start.2 = ((s32[8,48,1]{1,2,0:T(1,128)}), s32[8,48,1]{1,2,0:T(1,128)S(1)}, u32[]{:S(2)}, u32[]{:S(2)}) async-start(s32[8,48,1]{1,2,0:T(1,128)} %bitcast.14), calls=%async_computation.2 | async-start | bytes 8192 | tf_op jit(solution)/shard_map/all_to_all | solution.py:152
  71.6 17.8 %all-to-all-start.1 = ((s32[8,48,1]{1,2,0:T(1,128)}), s32[8,48,1]{1,2,0:T(1,128)S(1)}, u32[]{:S(2)}, u32[]{:S(2)}) async-start(s32[8,48,1]{1,2,0:T(1,128)} %bitcast.13), calls=%async_computation.1 | async-start | bytes 8192 | tf_op jit(solution)/shard_map/all_to_all | solution.py:153
  74.9 124.0 %reduce-scatter.2.cloned.1.call-start = ((), (), s32[]{:S(2)}) async-start(), calls=%async_computation.6 | async-start | bytes 1572864 | tf_op jit(solution)/shard_map/reduce_scatter | solution.py:163
  95.9 18.5 %collective-permute-start.2 = (bf16[1,48,2048]{2,1,0:T(8,128)(2,1)}, bf16[1,48,2048]{2,1,0:T(8,128)(2,1)S(1)}, u32[]{:S(2)}, u32[]{:S(2)}) collective-permute-start(bf16[1,48,2048]{2,1,0:T(8,128)(2,1)} %get-tuple-element.305), channel_id=1, source_target_pairs={{0,5},{1,8},{4,9},{5,12},{8,13},{9,0},{12,1},{13,4},{2,7},{3,10},{... | collective-permute-start | bytes 589832 | tf_op jit(solution)/shard_map/ppermute | solution.py:30
  96.0 18.5 %collective-permute-start.3 = (bf16[1,48,2048]{2,1,0:T(8,128)(2,1)S(1)}, bf16[1,48,2048]{2,1,0:T(8,128)(2,1)S(1)}, u32[]{:S(2)}, u32[]{:S(2)}) collective-permute-start(bf16[1,48,2048]{2,1,0:T(8,128)(2,1)S(1)} %get-tuple-element.304), channel_id=1, source_target_pairs={{0,8},{1,9},{4,12},{5,13},{8,0},{9,1},{12,4},{13,5},{2,10},{3,11},... | collective-permute-start | bytes 589832 | tf_op jit(solution)/shard_map/ppermute | solution.py:30
  97.0 17.6 %collective-permute-start.4 = (bf16[1,48,2048]{2,1,0:T(8,128)(2,1)S(1)}, bf16[1,48,2048]{2,1,0:T(8,128)(2,1)S(1)}, u32[]{:S(2)}, u32[]{:S(2)}) collective-permute-start(bf16[1,48,2048]{2,1,0:T(8,128)(2,1)S(1)} %get-tuple-element.303), channel_id=1, source_target_pairs={{0,9},{1,12},{4,13},{5,0},{8,1},{9,4},{12,5},{13,8},{2,11},{3,14},... | collective-permute-start | bytes 589832 | tf_op jit(solution)/shard_map/ppermute | solution.py:30
  99.3 15.3 %collective-permute-start.5 = (bf16[1,48,2048]{2,1,0:T(8,128)(2,1)S(1)}, bf16[1,48,2048]{2,1,0:T(8,128)(2,1)S(1)}, u32[]{:S(2)}, u32[]{:S(2)}) collective-permute-start(bf16[1,48,2048]{2,1,0:T(8,128)(2,1)S(1)} %get-tuple-element.302), channel_id=1, source_target_pairs={{0,12},{1,13},{4,0},{5,1},{8,4},{9,5},{12,8},{13,9},{2,14},{3,15},... | collective-permute-start | bytes 589832 | tf_op jit(solution)/shard_map/ppermute | solution.py:30
  102.2 14.1 %collective-permute-start.6 = (bf16[1,48,2048]{2,1,0:T(8,128)(2,1)S(1)}, bf16[1,48,2048]{2,1,0:T(8,128)(2,1)S(1)}, u32[]{:S(2)}, u32[]{:S(2)}) collective-permute-start(bf16[1,48,2048]{2,1,0:T(8,128)(2,1)S(1)} %get-tuple-element.301), channel_id=1, source_target_pairs={{0,13},{1,0},{4,1},{5,4},{8,5},{9,8},{12,9},{13,12},{2,15},{3,2},{... | collective-permute-start | bytes 589832 | tf_op jit(solution)/shard_map/ppermute | solution.py:30
Sparse Core Ops, SparseCore 0:
  12.7 30.5 all-gather.4
  46.7 28.4 all-gather.6
  168.5 30.3 reduce-scatter.1
